TPU v7x, 32 devices: a whole 2x2x4 slice. The times are simulated.
32 devices in a mesh: dp: 8 (over z, x), mp: 4 (over y, core).
Axes of the slice: x: 2, y: 2, z: 4, core: 2. Of those that a mesh axis runs over, the one named last changes fastest.
Arguments:
- activations: bfloat16 [4096, 3072], P('dp', 'mp'), may hold values from -6 to 6
- out_grads: bfloat16 [4096, 6144], P('dp', 'mp'), may hold values from -0.25 to 0.25
- error: bfloat16 [8, 3072, 6144], P('dp', 'mp'), may hold values from -8 to 8
- sketch: bfloat16 [6144, 64], replicated, may hold values from -0.078125 to 0.078125
- momentum: float32 [3072, 6144], P('mp', 'dp'), may hold values from -6 to 6
Outputs:
- error_new: bfloat16 [8, 3072, 6144], P('dp', 'mp')
- momentum_new: float32 [3072, 6144], P('mp', 'dp')
- next_sketch: bfloat16 [6144, 64], replicated
All inputs are finite; a program needn't handle non-finite values.
Results may differ from a plain program's by a relative error of at most 0.0057.
Values may be sent and summed in bfloat16 or wider, within the bound.
A program may use at most 64 MiB of HBM per device.

v0:
```python
import jax
import jax.numpy as jnp
from jax import lax
from jax.sharding import PartitionSpec as P

beta_decay = 0.9


def update_momentum(momentum, basis_rows, sketch_block):
    product = lax.dot_general(
        basis_rows, sketch_block, (((1,), (1,)), ((), ())), preferred_element_type=jnp.float32
    )
    return beta_decay * momentum + product


def local(activations, out_grads, error, sketch, momentum):
    own_error = error[0]
    product = lax.dot_general(
        activations,
        lax.all_gather(out_grads, "mp", axis=1, tiled=True),
        (((0,), (0,)), ((), ())),
        preferred_element_type=jnp.float32,
    )
    accumulated = (product + own_error.astype(jnp.float32)).astype(jnp.bfloat16)
    local_left = jnp.dot(accumulated, sketch, preferred_element_type=jnp.float32)
    left_sketch = lax.psum(local_left, "dp")
    gram_local = jnp.dot(
        left_sketch.T,
        left_sketch,
        precision=lax.Precision.HIGHEST,
        preferred_element_type=jnp.float32,
    )
    gram_matrix = lax.psum(gram_local, "mp")
    factor = jnp.linalg.cholesky(gram_matrix)
    basis_rows = jax.scipy.linalg.solve_triangular(factor, left_sketch.T, lower=True).T.astype(
        jnp.bfloat16
    )
    block_width = momentum.shape[1]
    local_right = lax.dot_general(
        accumulated, basis_rows, (((0,), (0,)), ((), ())), preferred_element_type=jnp.float32
    )
    right_sketch = lax.psum(local_right, ("dp", "mp"))
    next_sketch = right_sketch.astype(jnp.bfloat16)
    sketch_part = lax.dynamic_slice_in_dim(
        next_sketch, lax.axis_index("dp") * block_width, block_width, 0
    )
    momentum_new = update_momentum(momentum, basis_rows, sketch_part)
    decoded = lax.dot_general(
        basis_rows, next_sketch, (((1,), (1,)), ((), ())), preferred_element_type=jnp.float32
    )
    error_new = (accumulated.astype(jnp.float32) - decoded / lax.axis_size("dp")).astype(
        jnp.bfloat16
    )
    return (error_new[None], momentum_new, next_sketch)


def solution(mesh):
    in_specs = (P("dp", "mp"), P("dp", "mp"), P("dp", "mp", None), P(), P("mp", "dp"))
    out_specs = (P("dp", "mp", None), P("mp", "dp"), P())
    return jax.shard_map(local, mesh=mesh, in_specs=in_specs, out_specs=out_specs, check_vma=False)
```

profile of v0, /device:TPU:0, one launch (start us, length us, event | category | flops | bytes accessed | tf_op | source)
XLA Modules:
  0.0 249.4 jit_solution(14047941913646381180)
XLA Ops:
  7.2 0.0 copy-start
  7.2 0.0 all-gather.2.cloned.1.call-start
  7.2 0.7 all-gather.2.cloned.1.call-update
  7.9 0.0 copy-start.4
  7.9 0.0 all-reduce.3.cloned.1.call-start
  8.0 50.7 %all-gather.2.cloned.1.call-done = bf16[512,6144]{1,0:T(8,128)(2,1)} async-done(((bf16[512,1536]{1,0:T(8,128)(2,1)}), bf16[512,6144]{1,0:T(8,128)(2,1)}) %all-gather.2.cloned.1.call-update) | async-done | bytes 6291472 | tf_op jit(solution)/shard_map/all_gather | solution.py:20
  58.7 0.0 copy-done
  58.7 9.6 %fusion = bf16[768,6144]{1,0:T(8,128)(2,1)S(1)} fusion(bf16[1,768,6144]{2,1,0:T(8,128)(2,1)} %param.7, bf16[512,768]{1,0:T(8,128)(2,1)S(1)} %copy-done, bf16[512,6144]{1,0:T(8,128)(2,1)} %all-gather.2.cloned.1.call-done), kind=kOutput, calls=%fused_computation.1 | convolution fusion | flops 4845993984 | bytes 25952256 | tf_op jit(solution)/shard_map/dot_general | solution.py:18
  68.3 0.0 copy-start.1
  68.3 3.7 %copy-done.1 = bf16[768,6144]{1,0:T(8,128)(2,1)} copy-done((bf16[768,6144]{1,0:T(8,128)(2,1)}, bf16[768,6144]{1,0:T(8,128)(2,1)S(1)}, u32[]{:S(2)}) %copy-start.1) | copy-done | bytes 9437208
  72.1 0.0 copy-done.4
  72.1 3.7 %fusion.7 = f32[768,64]{0,1:T(8,128)} fusion(bf16[768,6144]{1,0:T(8,128)(2,1)S(1)} %fusion, bf16[6144,64]{0,1:T(8,128)(2,1)S(1)} %copy-done.4), kind=kOutput, calls=%fused_computation.17 | convolution fusion | flops 603979776 | bytes 10420224 | tf_op jit(solution)/shard_map/dot_general | solution.py:25
  75.7 0.0 all-reduce.3.cloned.1.call-update
  75.8 70.8 %all-reduce.3.cloned.1.call-done = f32[768,64]{0,1:T(8,128)} async-done(((f32[768,64]{0,1:T(8,128)}), f32[768,64]{0,1:T(8,128)}) %all-reduce.3.cloned.1.call-update) | async-done | bytes 196624 | tf_op jit(solution)/shard_map/psum | solution.py:26
  146.6 1.3 fusion.8
  147.9 10.3 %psum.22 = f32[64,64]{0,1:T(8,128)S(1)} all-reduce(f32[64,64]{0,1:T(8,128)S(1)} %fusion.8), channel_id=1, replica_groups=mesh['dp'=8,'mp'=4] {'mp'}, use_global_device_ids=true, to_apply=%region_1.0 | all-reduce | flops 4096 | bytes 32768 | tf_op jit(solution)/shard_map/psum | solution.py:33
  158.2 0.1 copy.9
  158.3 5.8 %cholesky.16 = f32[64,64]{1,0:T(8,128)S(1)} custom-call(f32[64,64]{1,0:T(8,128)S(1)} %fusion.5), custom_call_target="Cholesky" | custom-call | tf_op jit(solution)/shard_map/jit(cholesky)/cholesky | solution.py:34
  164.2 0.6 compare_reduce_fusion
  164.8 0.7 fusion.3
  165.5 4.9 %custom-call.7 = f32[1,64,64]{1,2,0:T(8,128)S(1)} custom-call(f32[1,64,64]{2,1,0:T(8,128)S(1)} %fusion.3), custom_call_target="InvertDiagBlocksLowerTriangular" | custom-call | tf_op jit(solution)/shard_map/jit(_solve_triangular)/triangular_solve | solution.py:35
  170.4 1.3 convolution_convert_fusion
  171.7 5.4 %fusion.9 = f32[6144,64]{0,1:T(8,128)S(1)} fusion(bf16[768,64]{0,1:T(8,128)(2,1)S(1)} %convolution_convert_fusion, bf16[768,6144]{1,0:T(8,128)(2,1)} %copy-done.1), kind=kOutput, calls=%fused_computation.19 | convolution fusion | flops 603979776 | bytes 11108352 | tf_op jit(solution)/shard_map/dot_general | solution.py:39
  177.1 55.7 %all-reduce.4 = bf16[6144,64]{0,1:T(8,128)(2,1)S(1)} all-reduce(f32[6144,64]{0,1:T(8,128)S(1)} %fusion.9), channel_id=1, replica_groups=mesh['dp'=8,'mp'=4] {'dp','mp'}, use_global_device_ids=true, to_apply=%region_4.5 | all-reduce | flops 393216 | bytes 2359296 | tf_op jit(solution)/shard_map/psum | solution.py:42
  232.8 0.0 copy-start.2
  232.8 0.0 copy-start.3
  232.8 7.8 %fusion.1 = bf16[1,768,6144]{2,1,0:T(8,128)(2,1)} fusion(bf16[768,64]{0,1:T(8,128)(2,1)S(1)} %convolution_convert_fusion, bf16[6144,64]{0,1:T(8,128)(2,1)S(1)} %all-reduce.4, bf16[768,6144]{1,0:T(8,128)(2,1)} %copy-done.1), kind=kOutput, calls=%fused_computation.3 | convolution fusion | flops 622854144 | bytes 19759104 | tf_op jit(solution)/shard_map/dot_general | solution.py:48
  240.7 0.0 copy-done.2
  240.7 0.0 copy-done.3
  240.7 1.9 multiply_add_fusion
  (2 shorter events, 0.0 us)
Async XLA Ops:
  7.2 51.5 %copy-start = (bf16[512,768]{1,0:T(8,128)(2,1)S(1)}, bf16[512,768]{1,0:T(8,128)(2,1)}, u32[]{:S(2)}) copy-start(bf16[512,768]{1,0:T(8,128)(2,1)} %param.5) | copy-start | bytes 2359300
  7.2 51.5 %all-gather.2.cloned.1.call-start = ((), (), s32[]{:S(2)}) async-start(), calls=%async_computation | async-start | bytes 7864320 | tf_op jit(solution)/shard_map/all_gather | solution.py:20
  7.9 64.2 %copy-start.4 = (bf16[6144,64]{0,1:T(8,128)(2,1)S(1)}, bf16[6144,64]{0,1:T(8,128)(2,1)}, u32[]{:S(2)}) copy-start(bf16[6144,64]{0,1:T(8,128)(2,1)} %param.8) | copy-start | bytes 2359300
  7.9 138.7 %all-reduce.3.cloned.1.call-start = ((), (), s32[]{:S(2)}) async-start(), calls=%async_computation.1 | async-start | bytes 393216 | tf_op jit(solution)/shard_map/psum | solution.py:26
  68.3 3.7 %copy-start.1 = (bf16[768,6144]{1,0:T(8,128)(2,1)}, bf16[768,6144]{1,0:T(8,128)(2,1)S(1)}, u32[]{:S(2)}) copy-start(bf16[768,6144]{1,0:T(8,128)(2,1)S(1)} %fusion) | copy-start | bytes 28311556
  232.8 7.8 %copy-start.2 = (bf16[6144,64]{0,1:T(8,128)(2,1)}, bf16[6144,64]{0,1:T(8,128)(2,1)S(1)}, u32[]{:S(2)}) copy-start(bf16[6144,64]{0,1:T(8,128)(2,1)S(1)} %all-reduce.4) | copy-start | bytes 2359300
  232.8 7.8 %copy-start.3 = (f32[768,768]{1,0:T(8,128)S(1)}, f32[768,768]{1,0:T(8,128)}, u32[]{:S(2)}) copy-start(f32[768,768]{1,0:T(8,128)} %param.9) | copy-start | bytes 7077892
Sparse Core Ops, SparseCore 0:
  9.5 49.0 all-gather.1
  75.9 70.6 all-reduce.2
where the time goes:
time: 250 us; the launch traced here: 249 us
  waiting for transfers between devices  122 us (49%)
  blocking collectives  66 us (26%)
  matrix products  31.1 us (12%)
  between operations  14.2 us (6%)
  other arithmetic  12.1 us (5%)
  local copies, waits for them, and re-layouts  3.84 us (2%)
    psum x1, waiting for transfers between devices, local(): left_sketch = lax.psum(local_left, 'dp')  70.8 us
    psum x1, blocking collectives, local(): right_sketch = lax.psum(local_right, ('dp', 'mp'))  55.7 us
    all_gather x1, waiting for transfers between devices, local(): lax.all_gather(out_grads, 'mp', axis=1, tiled=True)  50.7 us
    psum x1, blocking collectives, local(): gram_matrix = lax.psum(gram_local, 'mp')  10.3 us
    dot_general x1, matrix products, local(): lax.dot_general(activations, lax.all_gather(out_grads, 'mp', axis=1, tile...  9.64 us
    dot_general x1, matrix products, local(): lax.dot_general(basis_rows, next_sketch, (((1,), (1,)), ((), ())), prefer...  7.81 us
    another operation x3, other arithmetic, local(): factor = jnp.linalg.cholesky(gram_matrix)  6.52 us
    another operation x2, other arithmetic, local(): jax.scipy.linalg.solve_triangular(factor, left_sketch.T, lower=True)  5.55 us
  transfers between devices with their start and end apart: 2, of which 2 were waited for; matrix products, arithmetic and copies ran while one was open for 0% of the time, Pallas kernels for 0%

commit v1 on v0

v1 whole, which is shorter than its diff:
```python
import functools

import jax
import jax.numpy as jnp
from jax import lax
from jax.experimental import pallas as pl
from jax.experimental.pallas import tpu as pltpu
from jax.sharding import PartitionSpec as P

beta_decay = 0.9
F32, BF16 = jnp.float32, jnp.bfloat16
MESH = pl.DeviceIdType.MESH
HIGHEST = lax.Precision.HIGHEST


def native(activations, out_grads, error, sketch, momentum):
    product = lax.dot_general(
        activations,
        lax.all_gather(out_grads, "mp", axis=1, tiled=True),
        (((0,), (0,)), ((), ())),
        preferred_element_type=F32,
    )
    fed = (product + error[0].astype(F32)).astype(BF16)
    left = lax.psum(jnp.dot(fed, sketch, preferred_element_type=F32), "dp")
    gram = lax.psum(jnp.dot(left.T, left, precision=HIGHEST, preferred_element_type=F32), "mp")
    factor = jnp.linalg.cholesky(gram)
    basis = jax.scipy.linalg.solve_triangular(factor, left.T, lower=True).T.astype(BF16)
    right = lax.dot_general(fed, basis, (((0,), (0,)), ((), ())), preferred_element_type=F32)
    next_sketch = lax.psum(right, ("dp", "mp")).astype(BF16)
    width = momentum.shape[1]
    part = lax.dynamic_slice_in_dim(next_sketch, lax.axis_index("dp") * width, width, 0)
    momentum_new = beta_decay * momentum + lax.dot_general(
        basis, part, (((1,), (1,)), ((), ())), preferred_element_type=F32
    )
    decoded = lax.dot_general(
        basis, next_sketch, (((1,), (1,)), ((), ())), preferred_element_type=F32
    )
    error_new = (fed.astype(F32) - decoded / lax.axis_size("dp")).astype(BF16)
    return (error_new[None], momentum_new, next_sketch)


class Exchange:
    def __init__(self, axis, count, me, source, target, send_sem, recv_sem):
        self.axis, self.count, self.me = axis, count, me
        self.source, self.target = source, target
        self.send_sem, self.recv_sem = send_sem, recv_sem

    def copy(self, step, sender):
        peer = lax.rem(self.me + step, self.count)
        slot = self.me if sender else peer
        return pltpu.make_async_remote_copy(
            src_ref=self.source(peer),
            dst_ref=self.target(slot),
            send_sem=self.send_sem.at[step],
            recv_sem=self.recv_sem.at[slot],
            device_id={self.axis: peer},
            device_id_type=MESH,
        )

    def start(self):
        for step in range(1, self.count):
            self.copy(step, True).start()
        return self

    def wait(self):
        for step in range(1, self.count):
            self.copy(step, False).wait_recv()
        for step in range(1, self.count):
            self.copy(step, True).wait_send()


def total(slots, count):
    result = slots[0].astype(F32)
    for index in range(1, count):
        result = result + slots[index].astype(F32)
    return result


def inverse_factor(gram):
    rank = gram.shape[0]
    rows = lax.broadcasted_iota(jnp.int32, (rank, rank), 0)
    columns = lax.broadcasted_iota(jnp.int32, (rank, rank), 1)
    unit = (rows == columns).astype(F32)
    both = jnp.concatenate([gram, unit], axis=1)
    below = lax.broadcasted_iota(jnp.int32, (rank, 1), 0)
    for k in range(rank - 1):
        row = both[k : k + 1, :]
        scaled = row * (1.0 / row[:, k : k + 1])
        column = jnp.where(below > k, both[:, k : k + 1], 0.0)
        both = both - column * scaled
    pivots = jnp.sum(both[:, :rank] * unit, axis=1, keepdims=True)
    return both[:, rank:] * (1.0 / jnp.sqrt(pivots))


def chain_kernel(
    dp, mp, a_ref, g_ref, s_ref, e_hbm, basis_ref, sketch_ref,
    e_ref, gs, lf, lr, la, gm, ht, rt, rb, rr, qb, qr, nm,
    e_sem, mp_send, mp_recv, dp_send, dp_recv,
):
    me_d, me_m = lax.axis_index("dp"), lax.axis_index("mp")
    rows, width = e_ref.shape
    rank = s_ref.shape[1]
    columns = g_ref.shape[1]
    slab = rows // dp
    band = rank // mp
    block = width // dp

    def load(index):
        part = pl.ds(pl.multiple_of(index * slab, slab), slab)
        return pltpu.make_async_copy(e_hbm.at[0, part], e_ref.at[part], e_sem.at[index])

    for index in range(dp):
        load(index).start()

    barrier = pltpu.get_barrier_semaphore()
    for step in range(1, mp):
        pl.semaphore_signal(
            barrier, inc=1, device_id={"mp": lax.rem(me_m + step, mp)}, device_id_type=MESH
        )
    for step in range(1, dp):
        pl.semaphore_signal(
            barrier, inc=1, device_id={"dp": lax.rem(me_d + step, dp)}, device_id_type=MESH
        )
    pl.semaphore_wait(barrier, mp + dp - 2)

    mine = pl.ds(pl.multiple_of(me_m * columns, columns), columns)
    gs[me_m] = jnp.dot(g_ref[...], s_ref[mine, :], preferred_element_type=F32).T.astype(BF16)
    share = Exchange(
        "mp", mp, me_m, lambda p: gs.at[me_m], lambda p: gs.at[p], mp_send.at[0], mp_recv.at[0]
    ).start()

    def sketch_slab(index, carry):
        load(index).wait()
        part = pl.ds(pl.multiple_of(index * slab, slab), slab)
        lf[index] = jnp.dot(e_ref[part, :], s_ref[...], preferred_element_type=F32)
        return carry

    lax.fori_loop(0, dp, sketch_slab, 0)
    share.wait()
    grad_left = jnp.dot(total(gs, mp).astype(BF16), a_ref[...], preferred_element_type=F32).T
    lf[...] = lf[...] + grad_left.reshape(dp, slab, rank)

    share = Exchange(
        "dp", dp, me_d, lambda p: lf.at[p], lambda p: lr.at[p], dp_send.at[0], dp_recv.at[0]
    ).start()
    lr[me_d] = lf[me_d]
    share.wait()
    la[me_d] = total(lr, dp)
    share = Exchange(
        "dp", dp, me_d, lambda p: la.at[me_d], lambda p: la.at[p], dp_send.at[1], dp_recv.at[1]
    ).start()
    share.wait()
    left = la[...].reshape(rows, rank)
    gm[me_m] = jnp.dot(left.T, left, precision=HIGHEST, preferred_element_type=F32)
    share = Exchange(
        "mp", mp, me_m, lambda p: gm.at[me_m], lambda p: gm.at[p], mp_send.at[1], mp_recv.at[1]
    ).start()
    share.wait()
    inverse = inverse_factor(total(gm, mp))
    basis = jnp.dot(left, inverse.T, precision=HIGHEST, preferred_element_type=F32)
    basis_ref[...] = basis.astype(BF16)
    basis_t = basis.T.astype(BF16)

    ht[me_m] = jnp.dot(a_ref[...], basis_ref[...], preferred_element_type=F32).T.astype(BF16)
    share = Exchange(
        "mp", mp, me_m, lambda p: ht.at[me_m], lambda p: ht.at[p], mp_send.at[2], mp_recv.at[2]
    ).start()

    def right_block(index, carry):
        part = pl.ds(pl.multiple_of(index * block, block), block)
        rt[:, part] = jnp.dot(basis_t, e_ref[:, part], preferred_element_type=F32)
        return carry

    lax.fori_loop(0, dp, right_block, 0)
    share.wait()
    rt[:, mine] = rt[:, mine] + jnp.dot(
        total(ht, mp).astype(BF16), g_ref[...], preferred_element_type=F32
    )

    for index in range(mp):
        rb[index] = rt[index * band : (index + 1) * band, :].astype(BF16)
    share = Exchange(
        "mp", mp, me_m, lambda p: rb.at[p], lambda p: rr.at[p], mp_send.at[3], mp_recv.at[3]
    ).start()
    rr[me_m] = rb[me_m]
    share.wait()
    band_sum = total(rr, mp).astype(BF16)
    for index in range(dp):
        qb[index] = band_sum[:, index * block : (index + 1) * block]
    share = Exchange(
        "dp", dp, me_d, lambda p: qb.at[p], lambda p: qr.at[p], dp_send.at[2], dp_recv.at[2]
    ).start()
    qr[me_d] = qb[me_d]
    share.wait()
    nm[me_m, me_d] = total(qr, dp).astype(BF16)
    share = Exchange(
        "dp", dp, me_d, lambda p: nm.at[me_m, me_d], lambda p: nm.at[me_m, p],
        dp_send.at[3], dp_recv.at[3],
    ).start()
    share.wait()
    share = Exchange(
        "mp", mp, me_m, lambda p: nm.at[me_m], lambda p: nm.at[p], mp_send.at[4], mp_recv.at[4]
    ).start()
    share.wait()
    for m in range(mp):
        for d in range(dp):
            sketch_ref[m * band : (m + 1) * band, d * block : (d + 1) * block] = nm[m, d]


def finish_kernel(dp, a_ref, g_ref, e_ref, n_ref, b_ref, m_ref, error_ref, momentum_ref, turned):
    index = pl.program_id(0)

    @pl.when(index == 0)
    def _():
        turned[...] = a_ref[...].T

    product = jnp.dot(turned[...], g_ref[...], preferred_element_type=F32)
    fed = (product + e_ref[0].astype(F32)).astype(BF16)
    decoded = jnp.dot(b_ref[...], n_ref[...], preferred_element_type=F32)
    error_ref[0] = (fed.astype(F32) - decoded / dp).astype(BF16)

    @pl.when(index == lax.axis_index("dp"))
    def _():
        momentum_ref[...] = beta_decay * m_ref[...] + decoded


def step(dp, mp, activations, out_grads, error, sketch, momentum):
    tokens, rows = activations.shape
    columns = out_grads.shape[1]
    width, rank = sketch.shape
    block = momentum.shape[1]
    if rows % (16 * dp) or rank % (16 * mp) or block % 128 or columns % 128:
        return native(activations, out_grads, error, sketch, momentum)
    slab, band = rows // dp, rank // mp
    gathered = lax.all_gather(out_grads, "mp", axis=1, tiled=True)
    vmem = pl.BlockSpec(memory_space=pltpu.VMEM)
    basis, sketch_t = pl.pallas_call(
        functools.partial(chain_kernel, dp, mp),
        out_shape=(
            jax.ShapeDtypeStruct((rows, rank), BF16),
            jax.ShapeDtypeStruct((rank, width), BF16),
        ),
        in_specs=[vmem, vmem, vmem, pl.BlockSpec(memory_space=pl.ANY)],
        out_specs=(vmem, vmem),
        scratch_shapes=[
            pltpu.VMEM((rows, width), BF16),
            pltpu.VMEM((mp, rank, tokens), BF16),
            pltpu.VMEM((dp, slab, rank), F32),
            pltpu.VMEM((dp, slab, rank), F32),
            pltpu.VMEM((dp, slab, rank), F32),
            pltpu.VMEM((mp, rank, rank), F32),
            pltpu.VMEM((mp, rank, tokens), BF16),
            pltpu.VMEM((rank, width), F32),
            pltpu.VMEM((mp, band, width), BF16),
            pltpu.VMEM((mp, band, width), BF16),
            pltpu.VMEM((dp, band, block), BF16),
            pltpu.VMEM((dp, band, block), BF16),
            pltpu.VMEM((mp, dp, band, block), BF16),
            pltpu.SemaphoreType.DMA((dp,)),
            pltpu.SemaphoreType.DMA((5, mp)),
            pltpu.SemaphoreType.DMA((5, mp)),
            pltpu.SemaphoreType.DMA((4, dp)),
            pltpu.SemaphoreType.DMA((4, dp)),
        ],
        compiler_params=pltpu.CompilerParams(
            collective_id=0, has_side_effects=True, vmem_limit_bytes=56 << 20
        ),
        cost_estimate=pl.CostEstimate(
            flops=4 * rows * width * rank, bytes_accessed=8 * rows * width, transcendentals=0
        ),
        name="chain",
    )(activations, out_grads, sketch, error)
    whole = lambda shape: pl.BlockSpec(shape, lambda i: (0,) * len(shape))
    error_new, momentum_new = pl.pallas_call(
        functools.partial(finish_kernel, dp),
        grid=(dp,),
        out_shape=(
            jax.ShapeDtypeStruct(error.shape, BF16),
            jax.ShapeDtypeStruct(momentum.shape, F32),
        ),
        in_specs=[
            whole((tokens, rows)),
            pl.BlockSpec((tokens, block), lambda i: (0, i)),
            pl.BlockSpec((1, rows, block), lambda i: (0, 0, i)),
            pl.BlockSpec((rank, block), lambda i: (0, i)),
            whole((rows, rank)),
            whole((rows, block)),
        ],
        out_specs=(
            pl.BlockSpec((1, rows, block), lambda i: (0, 0, i)),
            whole((rows, block)),
        ),
        scratch_shapes=[pltpu.VMEM((rows, tokens), BF16)],
        compiler_params=pltpu.CompilerParams(
            dimension_semantics=("arbitrary",), vmem_limit_bytes=56 << 20
        ),
        name="finish",
    )(activations, gathered, error, sketch_t, basis, momentum)
    return (error_new, momentum_new, sketch_t.T)


def solution(mesh):
    body = functools.partial(step, mesh.shape["dp"], mesh.shape["mp"])
    in_specs = (P("dp", "mp"), P("dp", "mp"), P("dp", "mp", None), P(), P("mp", "dp"))
    out_specs = (P("dp", "mp", None), P("mp", "dp"), P())
    return jax.shard_map(body, mesh=mesh, in_specs=in_specs, out_specs=out_specs, check_vma=False)
```

time: 250 us -> 119 us (0.48)
  waiting for transfers between devices: 122 us -> 0.7 us
  Pallas kernels: 0 us -> 98.4 us
  blocking collectives: 66 us -> 0 us
  matrix products: 31.1 us -> 0 us
  other arithmetic: 12.1 us -> 0 us
    pallas_call x0 -> x2, Pallas kernels: none -> 98.4 us  [the longest x1 81.3 us: step(): pl.pallas_call(functools.partial(chain_kernel, dp, mp), out_shape=(jax.Sh...]
    psum x1 -> x0, waiting for transfers between devices: 70.8 us -> none  [local(): left_sketch = lax.psum(local_left, 'dp')]
    psum x2 -> x0, blocking collectives: 66 us -> none  [the longest x1 55.7 us: local(): right_sketch = lax.psum(local_right, ('dp', 'mp'))]
    all_gather x1, waiting for transfers between devices: 50.7 us -> 0.02 us  [step(): gathered = lax.all_gather(out_grads, 'mp', axis=1, tiled=True)]
    dot_general x6 -> x0, matrix products: 29.8 us -> none  [the longest x1 9.64 us: local(): lax.dot_general(activations, lax.all_gather(out_grads, 'mp', axis=1, tile...]
    another operation x5 -> x0, other arithmetic: 12.1 us -> none  [the longest x3 6.52 us: local(): factor = jnp.linalg.cholesky(gram_matrix)]
  transfers between devices with their start and end apart: 2 -> 1, of which waited for: 2 -> 0; matrix products, arithmetic and copies ran while one was open for 0% -> 2% of each run, Pallas kernels for 0% -> 70%
where the time goes in v1:
time: 119 us; the launch traced here: 117 us
  Pallas kernels  98.4 us (83%)
  between operations  14.1 us (12%)
  local copies, waits for them, and re-layouts  3.34 us (3%)
    pallas_call x1, Pallas kernels, step(): pl.pallas_call(functools.partial(chain_kernel, dp, mp), out_shape=(jax.Sh...  81.3 us
    pallas_call x1, Pallas kernels, step(): pl.pallas_call(functools.partial(finish_kernel, dp), grid=(dp,), out_shap...  17.1 us
    unnamed x4, local copies, waits for them, and re-layouts  3.34 us
  transfers between devices with their start and end apart: 1, of which 0 were waited for; matrix products, arithmetic and copies ran while one was open for 2% of the time, Pallas kernels for 70%

profile of v1, /device:TPU:0, one launch (start us, length us, event | category | flops | bytes accessed | tf_op | source)
XLA Modules:
  0.0 116.5 jit_solution(16337480186735307199)
XLA Ops:
  7.2 0.0 all-gather.2.cloned.1.call-start
  7.2 0.7 all-gather.2.cloned.1.call-update
  7.9 2.4 %copy.8.s_ref = bf16[6144,64]{1,0:T(8,128)(2,1)} copy(bf16[6144,64]{0,1:T(8,128)(2,1)} %param.8) | data formatting | bytes 1572864 | tf_op args[3]
  10.3 81.3 %chain.1 = (bf16[768,64]{1,0:T(8,128)(2,1)}, bf16[64,6144]{1,0:T(8,128)(2,1)}) custom-call(bf16[512,768]{1,0:T(8,128)(2,1)} %a_ref.3, bf16[512,1536]{1,0:T(8,128)(2,1)} %g_ref.1, bf16[6144,64]{1,0:T(8,128)(2,1)} %copy.8.s_ref, bf16[1,768,6144]{2,1,0:T(8,128)(2,1)} %e_ref.1), custom_call_target="tpu_custom_call" | custom-call | flops 1207959552 | bytes 37748736 | tf_op jit(solution)/shard_map/chain/pallas_call | solution.py:237
  91.7 0.0 all-gather.2.cloned.1.call-done.g_ref
  91.7 0.0 copy-start
  91.7 17.1 %finish.1 = (bf16[1,768,6144]{2,1,0:T(8,128)(2,1)}, f32[768,768]{1,0:T(8,128)}) custom-call(bf16[512,768]{1,0:T(8,128)(2,1)} %a_ref.3, bf16[512,6144]{1,0:T(8,128)(2,1)} %all-gather.2.cloned.1.call-done.g_ref, bf16[1,768,6144]{2,1,0:T(8,128)(2,1)} %e_ref.1, bf16[64,6144]{1,0:T(8,128)(2,1)} %get-tuple-element.7.n_ref, ...), custom_call_target="tpu_custom_call" | custom-call | tf_op jit(solution)/shard_map/finish/pallas_call | solution.py:274
  108.8 0.0 copy-done
  108.8 0.9 copy.10
Async XLA Ops:
  7.2 84.5 %all-gather.2.cloned.1.call-start = ((), (), s32[]{:S(2)}) async-start(), calls=%async_computation | async-start | bytes 7864320 | tf_op jit(solution)/shard_map/all_gather | solution.py:235
  91.7 17.1 %copy-start = (bf16[64,6144]{1,0:T(8,128)(2,1)S(1)}, bf16[64,6144]{1,0:T(8,128)(2,1)}, u32[]{:S(2)}) copy-start(bf16[64,6144]{1,0:T(8,128)(2,1)} %get-tuple-element.7.n_ref) | copy-start | bytes 2359300
Sparse Core Ops, SparseCore 0:
  9.5 54.3 all-gather.1

commit v2 on v1

--- a/solution.py
+++ b/solution.py
@@ -45,6 +45,9 @@
         self.source, self.target = source, target
         self.send_sem, self.recv_sem = send_sem, recv_sem
 
+    def place(self, peer):
+        return peer
+
     def copy(self, step, sender):
         peer = lax.rem(self.me + step, self.count)
         slot = self.me if sender else peer
@@ -53,7 +56,7 @@
             dst_ref=self.target(slot),
             send_sem=self.send_sem.at[step],
             recv_sem=self.recv_sem.at[slot],
-            device_id={self.axis: peer},
+            device_id={self.axis: self.place(peer)},
             device_id_type=MESH,
         )
 
@@ -62,11 +65,26 @@
             self.copy(step, True).start()
         return self
 
-    def wait(self):
+    def wait_recv(self):
         for step in range(1, self.count):
             self.copy(step, False).wait_recv()
+
+    def wait_send(self):
         for step in range(1, self.count):
             self.copy(step, True).wait_send()
+
+    def wait(self):
+        self.wait_recv()
+        self.wait_send()
+
+
+class Far(Exchange):
+    def __init__(self, chips, chip, core, source, target, send_sem, recv_sem):
+        super().__init__("mp", chips, chip, source, target, send_sem, recv_sem)
+        self.core = core
+
+    def place(self, peer):
+        return 2 * peer + self.core
 
 
 def total(slots, count):
@@ -93,13 +111,13 @@
 
 
 def chain_kernel(
-    dp, mp, a_ref, g_ref, s_ref, e_hbm, basis_ref, sketch_ref,
-    e_ref, gs, lf, lr, la, gm, ht, rt, rb, rr, qb, qr, nm,
-    e_sem, mp_send, mp_recv, dp_send, dp_recv,
+    dp, mp, a_ref, g_ref, st_ref, e_hbm, basis_ref, sketch_ref,
+    e_ref, s_ref, es, gs, lf, lr, la, gm, ht, rt, rb, rc, rd, ro, qb, qr, nm,
+    e_sem, mp_send, mp_recv, dp_send, dp_recv, pair_send, pair_recv, far_send, far_recv,
 ):
     me_d, me_m = lax.axis_index("dp"), lax.axis_index("mp")
     rows, width = e_ref.shape
-    rank = s_ref.shape[1]
+    rank = st_ref.shape[0]
     columns = g_ref.shape[1]
     slab = rows // dp
     band = rank // mp
@@ -123,6 +141,8 @@
         )
     pl.semaphore_wait(barrier, mp + dp - 2)
 
+    s_ref[...] = st_ref[...].T
+
     mine = pl.ds(pl.multiple_of(me_m * columns, columns), columns)
     gs[me_m] = jnp.dot(g_ref[...], s_ref[mine, :], preferred_element_type=F32).T.astype(BF16)
     share = Exchange(
@@ -132,13 +152,18 @@
     def sketch_slab(index, carry):
         load(index).wait()
         part = pl.ds(pl.multiple_of(index * slab, slab), slab)
-        lf[index] = jnp.dot(e_ref[part, :], s_ref[...], preferred_element_type=F32)
+        es[part, :] = jnp.dot(e_ref[part, :], s_ref[...], preferred_element_type=F32)
         return carry
 
     lax.fori_loop(0, dp, sketch_slab, 0)
     share.wait()
     grad_left = jnp.dot(total(gs, mp).astype(BF16), a_ref[...], preferred_element_type=F32).T
-    lf[...] = lf[...] + grad_left.reshape(dp, slab, rank)
+    local_left = es[...] + grad_left
+    half = slab // 2
+    for index in range(dp):
+        top = local_left[index * slab : index * slab + half]
+        low = local_left[index * slab + half : (index + 1) * slab]
+        lf[index] = jnp.concatenate([top, low], axis=1)
 
     share = Exchange(
         "dp", dp, me_d, lambda p: lf.at[p], lambda p: lr.at[p], dp_send.at[0], dp_recv.at[0]
@@ -150,7 +175,9 @@
         "dp", dp, me_d, lambda p: la.at[me_d], lambda p: la.at[p], dp_send.at[1], dp_recv.at[1]
     ).start()
     share.wait()
-    left = la[...].reshape(rows, rank)
+    left = jnp.concatenate(
+        [la[i][:, j * rank : (j + 1) * rank] for i in range(dp) for j in range(2)], axis=0
+    )
     gm[me_m] = jnp.dot(left.T, left, precision=HIGHEST, preferred_element_type=F32)
     share = Exchange(
         "mp", mp, me_m, lambda p: gm.at[me_m], lambda p: gm.at[p], mp_send.at[1], mp_recv.at[1]
@@ -177,31 +204,97 @@
         total(ht, mp).astype(BF16), g_ref[...], preferred_element_type=F32
     )
 
-    for index in range(mp):
-        rb[index] = rt[index * band : (index + 1) * band, :].astype(BF16)
-    share = Exchange(
-        "mp", mp, me_m, lambda p: rb.at[p], lambda p: rr.at[p], mp_send.at[3], mp_recv.at[3]
-    ).start()
-    rr[me_m] = rb[me_m]
-    share.wait()
-    band_sum = total(rr, mp).astype(BF16)
-    for index in range(dp):
-        qb[index] = band_sum[:, index * block : (index + 1) * block]
-    share = Exchange(
-        "dp", dp, me_d, lambda p: qb.at[p], lambda p: qr.at[p], dp_send.at[2], dp_recv.at[2]
-    ).start()
+    core, chip, chips = lax.rem(me_m, 2), me_m // 2, mp // 2
+    partner = me_m + 1 - 2 * core
+
+    def pair_copy(sem, d, source, target):
+        return pltpu.make_async_remote_copy(
+            src_ref=source,
+            dst_ref=target,
+            send_sem=pair_send.at[sem, d],
+            recv_sem=pair_recv.at[sem, d],
+            device_id={"mp": partner},
+            device_id_type=MESH,
+        )
+
+    def far(sem, d, source, target):
+        return Far(chips, chip, core, source, target, far_send.at[sem, d], far_recv.at[sem, d])
+
+    pairs, fars = [], []
+    for d in range(dp):
+        for m in range(mp):
+            rb[d, m % 2, m // 2] = rt[
+                m * band : (m + 1) * band, d * block : (d + 1) * block
+            ].astype(BF16)
+        pairs.append(pair_copy(0, d, rb.at[d, 1 - core], rc.at[d]))
+        pairs[-1].start()
+    for d in range(dp):
+        pairs[d].wait_recv()
+        rd[d] = (rb[d, core].astype(F32) + rc[d].astype(F32)).astype(BF16)
+        fars.append(far(0, d, lambda p, d=d: rd.at[d, p], lambda p, d=d: ro.at[d, p]))
+        fars[-1].start()
+        ro[d, chip] = rd[d, chip]
+    for d in range(dp):
+        fars[d].wait_recv()
+        qb[d] = total(ro.at[d], chips).astype(BF16)
+
+        @pl.when(me_d != d)
+        def _():
+            pltpu.make_async_remote_copy(
+                src_ref=qb.at[d],
+                dst_ref=qr.at[me_d],
+                send_sem=dp_send.at[2, d],
+                recv_sem=dp_recv.at[2, me_d],
+                device_id={"dp": d},
+                device_id_type=MESH,
+            ).start()
+
+    for each in pairs + fars:
+        each.wait_send()
     qr[me_d] = qb[me_d]
-    share.wait()
+    for step in range(1, dp):
+        peer = lax.rem(me_d + step, dp)
+        pltpu.make_async_remote_copy(
+            src_ref=qb.at[peer],
+            dst_ref=qr.at[peer],
+            send_sem=dp_send.at[2, peer],
+            recv_sem=dp_recv.at[2, peer],
+            device_id={"dp": peer},
+            device_id_type=MESH,
+        ).wait()
+
     nm[me_m, me_d] = total(qr, dp).astype(BF16)
     share = Exchange(
         "dp", dp, me_d, lambda p: nm.at[me_m, me_d], lambda p: nm.at[me_m, p],
         dp_send.at[3], dp_recv.at[3],
     ).start()
-    share.wait()
-    share = Exchange(
-        "mp", mp, me_m, lambda p: nm.at[me_m], lambda p: nm.at[p], mp_send.at[4], mp_recv.at[4]
-    ).start()
-    share.wait()
+    pairs, fars = [], []
+    for step in range(dp):
+        d = lax.rem(me_d + step, dp)
+        if step:
+            share.copy(step, False).wait_recv()
+        fars.append(
+            far(
+                1, step,
+                lambda p, d=d: nm.at[me_m, d],
+                lambda p, d=d: nm.at[2 * p + core, d],
+            ).start()
+        )
+        pairs.append(pair_copy(1, step, nm.at[me_m, d], nm.at[me_m, d]))
+        pairs[-1].start()
+    relays = []
+    for step in range(dp):
+        d = lax.rem(me_d + step, dp)
+        for hop in range(1, chips):
+            fars[step].copy(hop, False).wait_recv()
+            slot = 2 * lax.rem(chip + hop, chips) + core
+            relays.append(pair_copy(1 + hop, step, nm.at[slot, d], nm.at[slot, d]))
+            relays[-1].start()
+    for copy in pairs + relays:
+        copy.wait()
+    for each in fars:
+        each.wait_send()
+    share.wait_send()
     for m in range(mp):
         for d in range(dp):
             sketch_ref[m * band : (m + 1) * band, d * block : (d + 1) * block] = nm[m, d]
@@ -229,7 +322,7 @@
     columns = out_grads.shape[1]
     width, rank = sketch.shape
     block = momentum.shape[1]
-    if rows % (16 * dp) or rank % (16 * mp) or block % 128 or columns % 128:
+    if rows % (16 * dp) or rank % (16 * mp) or block % 128 or columns % 128 or mp % 2:
         return native(activations, out_grads, error, sketch, momentum)
     slab, band = rows // dp, rank // mp
     gathered = lax.all_gather(out_grads, "mp", axis=1, tiled=True)
@@ -244,15 +337,19 @@
         out_specs=(vmem, vmem),
         scratch_shapes=[
             pltpu.VMEM((rows, width), BF16),
+            pltpu.VMEM((width, rank), BF16),
+            pltpu.VMEM((rows, rank), F32),
             pltpu.VMEM((mp, rank, tokens), BF16),
-            pltpu.VMEM((dp, slab, rank), F32),
-            pltpu.VMEM((dp, slab, rank), F32),
-            pltpu.VMEM((dp, slab, rank), F32),
+            pltpu.VMEM((dp, slab // 2, 2 * rank), F32),
+            pltpu.VMEM((dp, slab // 2, 2 * rank), F32),
+            pltpu.VMEM((dp, slab // 2, 2 * rank), F32),
             pltpu.VMEM((mp, rank, rank), F32),
             pltpu.VMEM((mp, rank, tokens), BF16),
             pltpu.VMEM((rank, width), F32),
-            pltpu.VMEM((mp, band, width), BF16),
-            pltpu.VMEM((mp, band, width), BF16),
+            pltpu.VMEM((dp, 2, mp // 2, band, block), BF16),
+            pltpu.VMEM((dp, mp // 2, band, block), BF16),
+            pltpu.VMEM((dp, mp // 2, band, block), BF16),
+            pltpu.VMEM((dp, mp // 2, band, block), BF16),
             pltpu.VMEM((dp, band, block), BF16),
             pltpu.VMEM((dp, band, block), BF16),
             pltpu.VMEM((mp, dp, band, block), BF16),
@@ -261,6 +358,10 @@
             pltpu.SemaphoreType.DMA((5, mp)),
             pltpu.SemaphoreType.DMA((4, dp)),
             pltpu.SemaphoreType.DMA((4, dp)),
+            pltpu.SemaphoreType.DMA((1 + mp // 2, dp)),
+            pltpu.SemaphoreType.DMA((1 + mp // 2, dp)),
+            pltpu.SemaphoreType.DMA((2, dp, mp // 2)),
+            pltpu.SemaphoreType.DMA((2, dp, mp // 2)),
         ],
         compiler_params=pltpu.CompilerParams(
             collective_id=0, has_side_effects=True, vmem_limit_bytes=56 << 20
@@ -269,7 +370,7 @@
             flops=4 * rows * width * rank, bytes_accessed=8 * rows * width, transcendentals=0
         ),
         name="chain",
-    )(activations, out_grads, sketch, error)
+    )(activations, out_grads, sketch.T, error)
     whole = lambda shape: pl.BlockSpec(shape, lambda i: (0,) * len(shape))
     error_new, momentum_new = pl.pallas_call(
         functools.partial(finish_kernel, dp),

time: 119 us -> 106 us (0.89); the launches traced: 117 us -> 106 us
  Pallas kernels: 98.4 us -> 90.2 us
  local copies, waits for them, and re-layouts: 3.34 us -> 0.89 us
    pallas_call x1, Pallas kernels: 81.3 us -> 73.1 us  [step(): pl.pallas_call(functools.partial(chain_kernel, dp, mp), out_shape=(jax.Sh...]
    unnamed x4 -> x3, local copies, waits for them, and re-layouts: 3.34 us -> 0.89 us
  transfers between devices with their start and end apart: 1 -> 1, of which waited for: 0 -> 0; matrix products, arithmetic and copies ran while one was open for 2% -> 0% of each run, Pallas kernels for 70% -> 69%
where the time goes in v2:
time: 106 us
  Pallas kernels  90.2 us (85%)
  between operations  14.1 us (13%)
    pallas_call x1, Pallas kernels, step(): pl.pallas_call(functools.partial(chain_kernel, dp, mp), out_shape=(jax.Sh...  73.1 us
    pallas_call x1, Pallas kernels, step(): pl.pallas_call(functools.partial(finish_kernel, dp), grid=(dp,), out_shap...  17.1 us
  transfers between devices with their start and end apart: 1, of which 0 were waited for; matrix products, arithmetic and copies ran while one was open for 0% of the time, Pallas kernels for 69%

profile of v2, /device:TPU:0, one launch (start us, length us, event | category | flops | bytes accessed | tf_op | source)
XLA Modules:
  0.0 105.8 jit_solution(16512820623115655139)
XLA Ops:
  7.2 0.0 all-gather.2.cloned.1.call-start
  7.2 0.7 all-gather.2.cloned.1.call-update
  7.9 73.1 %chain.1 = (bf16[768,64]{1,0:T(8,128)(2,1)}, bf16[64,6144]{1,0:T(8,128)(2,1)}) custom-call(bf16[512,768]{1,0:T(8,128)(2,1)} %a_ref.3, bf16[512,1536]{1,0:T(8,128)(2,1)} %g_ref.1, bf16[64,6144]{1,0:T(8,128)(2,1)} %bitcast.3, bf16[1,768,6144]{2,1,0:T(8,128)(2,1)} %e_ref.1), custom_call_target="tpu_custom_call" | custom-call | flops 1207959552 | bytes 37748736 | tf_op jit(solution)/shard_map/chain/pallas_call | solution.py:330
  81.0 0.0 all-gather.2.cloned.1.call-done.g_ref
  81.0 0.0 copy-start
  81.0 17.1 %finish.1 = (bf16[1,768,6144]{2,1,0:T(8,128)(2,1)}, f32[768,768]{1,0:T(8,128)}) custom-call(bf16[512,768]{1,0:T(8,128)(2,1)} %a_ref.3, bf16[512,6144]{1,0:T(8,128)(2,1)} %all-gather.2.cloned.1.call-done.g_ref, bf16[1,768,6144]{2,1,0:T(8,128)(2,1)} %e_ref.1, bf16[64,6144]{1,0:T(8,128)(2,1)} %get-tuple-element.7.n_ref, ...), custom_call_target="tpu_custom_call" | custom-call | tf_op jit(solution)/shard_map/finish/pallas_call | solution.py:375
  98.1 0.0 copy-done
  98.1 0.9 copy.9
Async XLA Ops:
  7.2 73.9 %all-gather.2.cloned.1.call-start = ((), (), s32[]{:S(2)}) async-start(), calls=%async_computation | async-start | bytes 7864320 | tf_op jit(solution)/shard_map/all_gather | solution.py:328
  81.0 17.1 %copy-start = (bf16[64,6144]{1,0:T(8,128)(2,1)S(1)}, bf16[64,6144]{1,0:T(8,128)(2,1)}, u32[]{:S(2)}) copy-start(bf16[64,6144]{1,0:T(8,128)(2,1)} %get-tuple-element.7.n_ref) | copy-start | bytes 2359300
Sparse Core Ops, SparseCore 0:
  9.5 57.4 all-gather.1

commit v3 on v2

--- a/solution.py
+++ b/solution.py
@@ -8,6 +8,7 @@
 from jax.sharding import PartitionSpec as P
 
 beta_decay = 0.9
+CHUNKS = 8
 F32, BF16 = jnp.float32, jnp.bfloat16
 MESH = pl.DeviceIdType.MESH
 HIGHEST = lax.Precision.HIGHEST
@@ -111,9 +112,10 @@
 
 
 def chain_kernel(
-    dp, mp, a_ref, g_ref, st_ref, e_hbm, basis_ref, sketch_ref,
+    dp, mp, a_ref, g_ref, st_ref, e_hbm, basis_ref, sketch_ref, out_hbm,
     e_ref, s_ref, es, gs, lf, lr, la, gm, ht, rt, rb, rc, rd, ro, qb, qr, nm,
     e_sem, mp_send, mp_recv, dp_send, dp_recv, pair_send, pair_recv, far_send, far_recv,
+    gq, own_send, own_recv, y_send, y_recv, relay_send, relay_recv, out_sem,
 ):
     me_d, me_m = lax.axis_index("dp"), lax.axis_index("mp")
     rows, width = e_ref.shape
@@ -148,6 +150,53 @@
     share = Exchange(
         "mp", mp, me_m, lambda p: gs.at[me_m], lambda p: gs.at[p], mp_send.at[0], mp_recv.at[0]
     ).start()
+
+    core, chip, chips = lax.rem(me_m, 2), me_m // 2, mp // 2
+    partner = me_m + 1 - 2 * core
+    deep = g_ref.shape[0] // CHUNKS
+
+    def to_partner(source, slot, part, send_sem, recv_sem):
+        return pltpu.make_async_remote_copy(
+            src_ref=source.at[part],
+            dst_ref=gq.at[slot, part],
+            send_sem=send_sem,
+            recv_sem=recv_sem,
+            device_id={"mp": partner},
+            device_id_type=MESH,
+        )
+
+    everything = pl.ds(0, g_ref.shape[0])
+    own = to_partner(g_ref, me_m, everything, own_send.at[0], own_recv.at[0])
+    own.start()
+    kept = pltpu.make_async_copy(g_ref, out_hbm.at[me_m], out_sem.at[me_m])
+    kept.start()
+    chunk_parts = [pl.ds(c * deep, deep) for c in range(CHUNKS)]
+    chunks = [
+        Far(
+            chips, chip, core,
+            lambda p, part=part: g_ref.at[part],
+            lambda p, part=part: gq.at[2 * p + core, part],
+            y_send.at[c], y_recv.at[c],
+        )
+        for c, part in enumerate(chunk_parts)
+    ]
+    relayed = []
+
+    def relay(first, last):
+        for c in range(first, last):
+            for hop in range(1, chips):
+                chunks[c].copy(hop, False).wait_recv()
+                slot = 2 * lax.rem(chip + hop, chips) + core
+                relayed.append(
+                    to_partner(
+                        gq.at[slot], slot, chunk_parts[c],
+                        relay_send.at[c, hop], relay_recv.at[c, hop],
+                    )
+                )
+                relayed[-1].start()
+
+    for c in range(CHUNKS // 2):
+        chunks[c].start()
 
     def sketch_slab(index, carry):
         load(index).wait()
@@ -183,6 +232,9 @@
         "mp", mp, me_m, lambda p: gm.at[me_m], lambda p: gm.at[p], mp_send.at[1], mp_recv.at[1]
     ).start()
     share.wait()
+    mid = CHUNKS // 2
+    chunks[mid].start()
+    relay(0, mid)
     inverse = inverse_factor(total(gm, mp))
     basis = jnp.dot(left, inverse.T, precision=HIGHEST, preferred_element_type=F32)
     basis_ref[...] = basis.astype(BF16)
@@ -192,6 +244,7 @@
     share = Exchange(
         "mp", mp, me_m, lambda p: ht.at[me_m], lambda p: ht.at[p], mp_send.at[2], mp_recv.at[2]
     ).start()
+    chunks[mid + 1].start()
 
     def right_block(index, carry):
         part = pl.ds(pl.multiple_of(index * block, block), block)
@@ -203,9 +256,6 @@
     rt[:, mine] = rt[:, mine] + jnp.dot(
         total(ht, mp).astype(BF16), g_ref[...], preferred_element_type=F32
     )
-
-    core, chip, chips = lax.rem(me_m, 2), me_m // 2, mp // 2
-    partner = me_m + 1 - 2 * core
 
     def pair_copy(sem, d, source, target):
         return pltpu.make_async_remote_copy(
@@ -234,6 +284,9 @@
         fars.append(far(0, d, lambda p, d=d: rd.at[d, p], lambda p, d=d: ro.at[d, p]))
         fars[-1].start()
         ro[d, chip] = rd[d, chip]
+    for c in range(mid + 2, CHUNKS):
+        chunks[c].start()
+    relay(mid, mid + 2)
     for d in range(dp):
         fars[d].wait_recv()
         qb[d] = total(ro.at[d], chips).astype(BF16)
@@ -282,6 +335,15 @@
         )
         pairs.append(pair_copy(1, step, nm.at[me_m, d], nm.at[me_m, d]))
         pairs[-1].start()
+    relay(mid + 2, CHUNKS)
+    own.wait()
+    for each in chunks:
+        each.wait_send()
+    for copy in relayed:
+        copy.wait()
+    for hop in range(1, mp):
+        slot = lax.rem(me_m + hop, mp)
+        pltpu.make_async_copy(gq.at[slot], out_hbm.at[slot], out_sem.at[slot]).start()
     relays = []
     for step in range(dp):
         d = lax.rem(me_d + step, dp)
@@ -295,6 +357,10 @@
     for each in fars:
         each.wait_send()
     share.wait_send()
+    for hop in range(1, mp):
+        slot = lax.rem(me_m + hop, mp)
+        pltpu.make_async_copy(gq.at[slot], out_hbm.at[slot], out_sem.at[slot]).wait()
+    kept.wait()
     for m in range(mp):
         for d in range(dp):
             sketch_ref[m * band : (m + 1) * band, d * block : (d + 1) * block] = nm[m, d]
@@ -307,7 +373,7 @@
     def _():
         turned[...] = a_ref[...].T
 
-    product = jnp.dot(turned[...], g_ref[...], preferred_element_type=F32)
+    product = jnp.dot(turned[...], g_ref[0], preferred_element_type=F32)
     fed = (product + e_ref[0].astype(F32)).astype(BF16)
     decoded = jnp.dot(b_ref[...], n_ref[...], preferred_element_type=F32)
     error_ref[0] = (fed.astype(F32) - decoded / dp).astype(BF16)
@@ -322,19 +388,19 @@
     columns = out_grads.shape[1]
     width, rank = sketch.shape
     block = momentum.shape[1]
-    if rows % (16 * dp) or rank % (16 * mp) or block % 128 or columns % 128 or mp % 2:
+    if rows % (16 * dp) or rank % (16 * mp) or block % 128 or columns % block or mp % 2 or tokens % (16 * CHUNKS):
         return native(activations, out_grads, error, sketch, momentum)
     slab, band = rows // dp, rank // mp
-    gathered = lax.all_gather(out_grads, "mp", axis=1, tiled=True)
     vmem = pl.BlockSpec(memory_space=pltpu.VMEM)
-    basis, sketch_t = pl.pallas_call(
+    basis, sketch_t, gathered = pl.pallas_call(
         functools.partial(chain_kernel, dp, mp),
         out_shape=(
             jax.ShapeDtypeStruct((rows, rank), BF16),
             jax.ShapeDtypeStruct((rank, width), BF16),
+            jax.ShapeDtypeStruct((mp, tokens, columns), BF16),
         ),
         in_specs=[vmem, vmem, vmem, pl.BlockSpec(memory_space=pl.ANY)],
-        out_specs=(vmem, vmem),
+        out_specs=(vmem, vmem, pl.BlockSpec(memory_space=pl.ANY)),
         scratch_shapes=[
             pltpu.VMEM((rows, width), BF16),
             pltpu.VMEM((width, rank), BF16),
@@ -362,6 +428,14 @@
             pltpu.SemaphoreType.DMA((1 + mp // 2, dp)),
             pltpu.SemaphoreType.DMA((2, dp, mp // 2)),
             pltpu.SemaphoreType.DMA((2, dp, mp // 2)),
+            pltpu.VMEM((mp, tokens, columns), BF16),
+            pltpu.SemaphoreType.DMA((1,)),
+            pltpu.SemaphoreType.DMA((1,)),
+            pltpu.SemaphoreType.DMA((CHUNKS, mp // 2)),
+            pltpu.SemaphoreType.DMA((CHUNKS, mp // 2)),
+            pltpu.SemaphoreType.DMA((CHUNKS, mp // 2)),
+            pltpu.SemaphoreType.DMA((CHUNKS, mp // 2)),
+            pltpu.SemaphoreType.DMA((mp,)),
         ],
         compiler_params=pltpu.CompilerParams(
             collective_id=0, has_side_effects=True, vmem_limit_bytes=56 << 20
@@ -371,6 +445,7 @@
         ),
         name="chain",
     )(activations, out_grads, sketch.T, error)
+    per = columns // block
     whole = lambda shape: pl.BlockSpec(shape, lambda i: (0,) * len(shape))
     error_new, momentum_new = pl.pallas_call(
         functools.partial(finish_kernel, dp),
@@ -381,7 +456,7 @@
         ),
         in_specs=[
             whole((tokens, rows)),
-            pl.BlockSpec((tokens, block), lambda i: (0, i)),
+            pl.BlockSpec((1, tokens, block), lambda i: (i // per, 0, i % per)),
             pl.BlockSpec((1, rows, block), lambda i: (0, 0, i)),
             pl.BlockSpec((rank, block), lambda i: (0, i)),
             whole((rows, rank)),

time: 106 us -> 89.9 us (0.85)
  between operations: 14.1 us -> 0.65 us
  Pallas kernels: 90.2 us -> 88 us
    pallas_call x1, Pallas kernels: 73.1 us -> 70.8 us  [step(): pl.pallas_call(functools.partial(chain_kernel, dp, mp), out_shape=(jax.Sh...]
  transfers between devices with their start and end apart: 1 -> 0, of which waited for: 0 -> 0; matrix products, arithmetic and copies ran while one was open for 0% -> 0% of each run, Pallas kernels for 69% -> 0%
where the time goes in v3:
time: 89.9 us; the launch traced here: 89.6 us
  Pallas kernels  88 us (98%)
    pallas_call x1, Pallas kernels, step(): pl.pallas_call(functools.partial(chain_kernel, dp, mp), out_shape=(jax.Sh...  70.8 us
    pallas_call x1, Pallas kernels, step(): pl.pallas_call(functools.partial(finish_kernel, dp), grid=(dp,), out_shap...  17.2 us

profile of v3, /device:TPU:0, one launch (start us, length us, event | category | flops | bytes accessed | tf_op | source)
XLA Modules:
  0.0 89.6 jit_solution(8450023741561712904)
XLA Ops:
  0.6 70.8 %chain.1 = (bf16[768,64]{1,0:T(8,128)(2,1)}, bf16[64,6144]{1,0:T(8,128)(2,1)}, bf16[4,512,1536]{2,1,0:T(8,128)(2,1)}) custom-call(bf16[512,768]{1,0:T(8,128)(2,1)} %a_ref.3, bf16[512,1536]{1,0:T(8,128)(2,1)} %g_ref.1, bf16[64,6144]{1,0:T(8,128)(2,1)} %bitcast.3, bf16[1,768,6144]{2,1,0:T(8,128)(2,1)} %e_ref.1), custom_call_target="tpu_custom_call" | custom-call | flops 1207959552 | bytes 37748736 | tf_op jit(solution)/shard_map/chain/pallas_call | solution.py:395
  71.5 0.0 copy-start
  71.5 17.2 %finish.1 = (bf16[1,768,6144]{2,1,0:T(8,128)(2,1)}, f32[768,768]{1,0:T(8,128)}) custom-call(bf16[512,768]{1,0:T(8,128)(2,1)} %a_ref.3, bf16[4,512,1536]{2,1,0:T(8,128)(2,1)} %get-tuple-element.8.g_ref, bf16[1,768,6144]{2,1,0:T(8,128)(2,1)} %e_ref.1, bf16[64,6144]{1,0:T(8,128)(2,1)} %get-tuple-element.9.n_ref, bf16[768,64]{1,0:T(8,128)(2,1)} %get-tuple-element.10.b_ref, ...), custom_call_target="tpu_custom_call" | custom-call | tf_op jit(solution)/shard_map/finish/pallas_call | solution.py:450
  88.7 0.0 copy-done
  88.7 0.9 copy.9
Async XLA Ops:
  71.5 17.2 %copy-start = (bf16[64,6144]{1,0:T(8,128)(2,1)S(1)}, bf16[64,6144]{1,0:T(8,128)(2,1)}, u32[]{:S(2)}) copy-start(bf16[64,6144]{1,0:T(8,128)(2,1)} %get-tuple-element.9.n_ref) | copy-start | bytes 2359300
